TPU v7x, 128 devices: a whole 4x4x4 slice. The times are simulated.
128 devices in a mesh: row: 16 (over y, z), col: 8 (over x, core).
Axes of the slice: x: 4, y: 4, z: 4, core: 2. Of those that a mesh axis runs over, the one named last changes fastest.
Arguments:
- tokens: bfloat16 [2048, 4096], P('row', 'col'), may hold values from -6 to 6
- w_in: bfloat16 [4096, 16384], P('col', 'row'), may hold values from -0.09375 to 0.09375
- w_out: bfloat16 [16384, 4096], P('row', 'col'), may hold values from -0.046875 to 0.046875
- cotangent: bfloat16 [2048, 4096], P('row', 'col'), may hold values from -6 to 6
Outputs:
- block_out: bfloat16 [2048, 4096], P(('row', 'col'))
- grad_tokens: bfloat16 [2048, 4096], P('row', 'col')
- grad_in: float32 [4096, 16384], P('col', 'row')
- grad_out: float32 [16384, 4096], P('row', 'col')
All inputs are finite; a program needn't handle non-finite values.
Results may differ from a plain program's by a relative error of at most 0.015.
Values may be sent and summed in bfloat16 or wider, within the bound.
A program may use at most 128 MiB of HBM per device.

v0:
```python
import jax
import jax.numpy as jnp
from jax import lax
from jax.sharding import PartitionSpec as P


def gelu_grad(value):
    cdf = 0.5 * (1.0 + jax.scipy.special.erf(value * 0.7071067811865476))
    pdf = jnp.exp(-0.5 * value * value) * 0.3989422804014327
    return cdf + value * pdf


def token_panel(local_rows):
    return lax.all_gather(local_rows, "row", axis=0, tiled=True)


def token_panel_a2a(local_rows):
    n = lax.axis_size("row")
    copies = jnp.broadcast_to(local_rows[None], (n,) + local_rows.shape)
    copies = copies.reshape(n * local_rows.shape[0], local_rows.shape[1])
    return lax.all_to_all(copies, "row", split_axis=0, concat_axis=0, tiled=True)


def hidden_panel(local_rows):
    return lax.all_gather(local_rows, "col", axis=0, tiled=True)


def contract_last(left, right):
    return lax.dot_general(
        left, right, (((1,), (1,)), ((), ())), preferred_element_type=jnp.float32
    )


def width_split(left_all, right, transposed):
    if transposed:
        term = contract_last(left_all, right)
    else:
        term = jnp.dot(left_all, right, preferred_element_type=jnp.float32)
    return lax.psum_scatter(
        term.astype(jnp.bfloat16), "col", scatter_dimension=0, tiled=True
    ).astype(jnp.float32)


def unit_sum(left_all, right, transposed):
    n = lax.axis_size("row")
    if transposed:
        term = contract_last(left_all, right)
    else:
        term = jnp.dot(left_all, right, preferred_element_type=jnp.float32)
    pieces = term.astype(jnp.bfloat16).reshape(n, term.shape[0] // n, term.shape[1])
    pieces = lax.all_to_all(pieces, "row", split_axis=0, concat_axis=0, tiled=True)
    return jnp.sum(pieces.astype(jnp.float32), axis=0)


def local(tokens, w_in, w_out, cotangent):
    tokens_all = token_panel(tokens)
    upstream_all = token_panel_a2a(cotangent)
    pre_part = width_split(tokens_all, w_in, False)
    act_all = hidden_panel(jax.nn.gelu(pre_part, approximate=False).astype(jnp.bfloat16))
    dact_part = width_split(upstream_all, w_out, True)
    dpre_all = hidden_panel((dact_part * gelu_grad(pre_part)).astype(jnp.bfloat16))
    mixed = unit_sum(act_all, w_out, False)
    block_rows = (tokens.astype(jnp.float32) + mixed).astype(jnp.bfloat16)
    block_out = lax.all_to_all(block_rows, "col", split_axis=0, concat_axis=1, tiled=True)
    grad_out = lax.dot_general(
        act_all, upstream_all, (((0,), (0,)), ((), ())), preferred_element_type=jnp.float32
    )
    grad_in = lax.dot_general(
        tokens_all, dpre_all, (((0,), (0,)), ((), ())), preferred_element_type=jnp.float32
    )
    back = unit_sum(dpre_all, w_in, True)
    grad_tokens = (cotangent.astype(jnp.float32) + back).astype(jnp.bfloat16)
    return (block_out, grad_tokens, grad_in, grad_out)


def solution(mesh):
    in_specs = (P("row", "col"), P("col", "row"), P("row", "col"), P("row", "col"))
    out_specs = (P(("row", "col"), None), P("row", "col"), P("col", "row"), P("row", "col"))
    return jax.shard_map(local, mesh=mesh, in_specs=in_specs, out_specs=out_specs, check_vma=False)
```

profile of v0, /device:TPU:1, one launch (start us, length us, event | category | flops | bytes accessed | tf_op | source)
XLA Modules:
  0.0 260.2 jit_solution(16874489885100301524)
XLA Ops:
  8.0 0.0 copy-start
  8.0 0.0 all-gather.4.cloned.1.call-start
  8.1 0.7 all-gather.4.cloned.1.call-update
  8.7 0.0 reduce-scatter.5.cloned.1.call-start
  8.8 1.1 broadcast_in_dim.2
  9.9 37.6 %all_to_all.38 = bf16[16,128,512]{2,1,0:T(8,128)(2,1)S(1)} all-to-all(bf16[16,128,512]{2,1,0:T(8,128)(2,1)S(1)} %broadcast_in_dim.2), channel_id=1, replica_groups=mesh['row'=16,'col'=8] {'row'}, dimensions={0} | all-to-all | bytes 4194304 | tf_op jit(solution)/shard_map/all_to_all | solution.py:21
  47.5 0.0 copy-start.1
  47.5 1.4 copy-done.1
  48.9 0.0 copy-done
  48.9 4.3 %convolution_convert_fusion = bf16[2048,1024]{1,0:T(8,128)(2,1)} fusion(bf16[2048,512]{1,0:T(8,128)(2,1)S(1)} %bitcast.21, bf16[1024,512]{1,0:T(8,128)(2,1)S(1)} %copy-done), kind=kOutput, calls=%fused_computation.2 | convolution fusion | flops 2149580800 | bytes 7340032 | tf_op jit(solution)/shard_map/dot_general | solution.py:29
  53.2 0.0 copy-start.4
  53.2 0.0 reduce-scatter.5.cloned.1.call-update
  53.3 0.0 reduce-scatter.3.cloned.1.call-start
  53.3 12.5 %all-gather.4.cloned.1.call-done = bf16[2048,512]{1,0:T(8,128)(2,1)} async-done(((bf16[128,512]{1,0:T(8,128)(2,1)}), bf16[2048,512]{1,0:T(8,128)(2,1)}) %all-gather.4.cloned.1.call-update) | async-done | bytes 2097168 | tf_op jit(solution)/shard_map/all_gather | solution.py:14
  65.8 0.0 copy-done.4
  65.8 5.9 %convolution_convert_fusion.1 = bf16[2048,1024]{1,0:T(8,128)(2,1)} fusion(bf16[2048,512]{1,0:T(8,128)(2,1)} %all-gather.4.cloned.1.call-done, bf16[512,1024]{1,0:T(8,128)(2,1)S(1)} %copy-done.4), kind=kOutput, calls=%fused_computation.3 | convolution fusion | flops 2149580800 | bytes 7340032 | tf_op jit(solution)/shard_map/dot_general | solution.py:38
  71.8 0.0 reduce-scatter.3.cloned.1.call-update
  71.8 0.0 all-gather.6.cloned.1.call-start
  71.9 15.8 %reduce-scatter.5.cloned.1.call-done = bf16[256,1024]{1,0:T(8,128)(2,1)} async-done(((bf16[2048,1024]{1,0:T(8,128)(2,1)}), bf16[256,1024]{1,0:T(8,128)(2,1)}) %reduce-scatter.5.cloned.1.call-update) | async-done | bytes 524304 | tf_op jit(solution)/shard_map/reduce_scatter | solution.py:39
  87.7 38.8 %reduce-scatter.3.cloned.1.call-done = bf16[256,1024]{1,0:T(8,128)(2,1)} async-done(((bf16[2048,1024]{1,0:T(8,128)(2,1)}), bf16[256,1024]{1,0:T(8,128)(2,1)}) %reduce-scatter.3.cloned.1.call-update) | async-done | bytes 524304 | tf_op jit(solution)/shard_map/reduce_scatter | solution.py:39
  126.4 4.6 %fusion.38 = (bf16[256,1024]{1,0:T(8,128)(2,1)}, bf16[256,1024]{1,0:T(8,128)(2,1)}) fusion(bf16[256,1024]{1,0:T(8,128)(2,1)} %reduce-scatter.3.cloned.1.call-done, bf16[256,1024]{1,0:T(8,128)(2,1)} %reduce-scatter.5.cloned.1.call-done), kind=kLoop, calls=%fused_computation.52 | loop fusion | flops 20185088 | bytes 2097152 | tf_op jit(solution)/shard_map/convert_element_type | solution.py:61
  131.0 0.0 all-gather.6.cloned.1.call-update
  131.0 0.0 all-gather.8.cloned.1.call-start
  131.1 0.7 all-gather.8.cloned.1.call-update
  131.8 33.5 %all-gather.6.cloned.1.call-done = bf16[2048,1024]{1,0:T(8,128)(2,1)} async-done(((bf16[256,1024]{1,0:T(8,128)(2,1)}), bf16[2048,1024]{1,0:T(8,128)(2,1)}) %all-gather.6.cloned.1.call-update) | async-done | bytes 4194320 | tf_op jit(solution)/shard_map/all_gather | solution.py:25
  165.3 5.8 %convolution_convert_fusion.3 = bf16[2048,512]{1,0:T(8,128)(2,1)} fusion(bf16[2048,1024]{1,0:T(8,128)(2,1)} %all-gather.6.cloned.1.call-done, bf16[1024,512]{1,0:T(8,128)(2,1)S(1)} %copy-done), kind=kOutput, calls=%fused_computation.5 | convolution fusion | flops 2148532224 | bytes 7340032 | tf_op jit(solution)/shard_map/dot_general | solution.py:49
  171.1 6.7 %all-to-all-start = ((bf16[16,128,512]{2,1,0:T(8,128)(2,1)}), bf16[16,128,512]{2,1,0:T(8,128)(2,1)S(1)}, u32[]{:S(2)}, u32[]{:S(2)}) async-start(bf16[16,128,512]{2,1,0:T(8,128)(2,1)} %bitcast.24), calls=%async_computation.1 | async-start | bytes 4194304 | tf_op jit(solution)/shard_map/all_to_all | solution.py:51
  177.9 21.7 %all-gather.8.cloned.1.call-done = bf16[2048,1024]{1,0:T(8,128)(2,1)} async-done(((bf16[256,1024]{1,0:T(8,128)(2,1)}), bf16[2048,1024]{1,0:T(8,128)(2,1)}) %all-gather.8.cloned.1.call-update) | async-done | bytes 4194320 | tf_op jit(solution)/shard_map/all_gather | solution.py:25
  199.5 6.2 %convolution_convert_fusion.2 = bf16[2048,512]{1,0:T(8,128)(2,1)} fusion(bf16[2048,1024]{1,0:T(8,128)(2,1)} %all-gather.8.cloned.1.call-done, bf16[512,1024]{1,0:T(8,128)(2,1)} %param.5), kind=kOutput, calls=%fused_computation.4 | convolution fusion | flops 2148532224 | bytes 7340032 | tf_op jit(solution)/shard_map/dot_general | solution.py:29
  205.7 1.4 all-to-all-done
  207.1 5.4 %all-to-all-start.3 = ((bf16[16,128,512]{2,1,0:T(8,128)(2,1)}), bf16[16,128,512]{2,1,0:T(8,128)(2,1)}, u32[]{:S(2)}, u32[]{:S(2)}) async-start(bf16[16,128,512]{2,1,0:T(8,128)(2,1)} %bitcast.23), calls=%async_computation.5 | async-start | bytes 4194304 | tf_op jit(solution)/shard_map/all_to_all | solution.py:51
  212.5 6.6 %convolution_bitcast_fusion = f32[512,1024]{0,1:T(8,128)} fusion(bf16[2048,1024]{1,0:T(8,128)(2,1)} %all-gather.8.cloned.1.call-done, bf16[2048,512]{1,0:T(8,128)(2,1)} %all-gather.4.cloned.1.call-done), kind=kOutput, calls=%fused_computation.12 | convolution fusion | flops 2147483648 | bytes 8388608 | tf_op jit(solution)/shard_map/dot_general | solution.py:68
  219.0 2.9 %copy.12 = f32[512,1024]{1,0:T(8,128)} copy(f32[512,1024]{0,1:T(8,128)} %convolution_bitcast_fusion) | data formatting | bytes 4194304
  221.9 6.5 %fusion.39 = f32[1024,512]{1,0:T(8,128)} fusion(bf16[2048,1024]{1,0:T(8,128)(2,1)} %all-gather.6.cloned.1.call-done, bf16[2048,512]{1,0:T(8,128)(2,1)} %bitcast.22), kind=kOutput, calls=%fused_computation.55 | convolution fusion | flops 2147483648 | bytes 8388608 | tf_op jit(solution)/shard_map/dot_general | solution.py:65
  228.5 0.0 copy-start.3
  228.5 0.3 convert_reduce_fusion.1
  228.8 0.6 copy-done.3
  229.4 0.0 copy-start.2
  229.4 0.7 add_convert_fusion.1
  230.0 8.0 %all-to-all-done.3 = bf16[16,128,512]{2,1,0:T(8,128)(2,1)} async-done(((bf16[16,128,512]{2,1,0:T(8,128)(2,1)}), bf16[16,128,512]{2,1,0:T(8,128)(2,1)}, u32[]{:S(2)}, u32[]{:S(2)}) %all-to-all-start.3) | async-done | bytes 2097184 | tf_op jit(solution)/shard_map/all_to_all | solution.py:51
  238.1 8.6 %all-to-all-start.1 = ((bf16[8,16,512]{2,1,0:T(8,128)(2,1)}), bf16[8,16,512]{2,1,0:T(8,128)(2,1)S(1)}, u32[]{:S(2)}, u32[]{:S(2)}) async-start(bf16[8,16,512]{2,1,0:T(8,128)(2,1)} %bitcast.1), calls=%async_computation.2 | async-start | bytes 262144 | tf_op jit(solution)/shard_map/all_to_all | solution.py:64
  246.7 1.9 convert_reduce_fusion
  248.6 0.0 copy-done.2
  248.6 0.7 add_convert_fusion
  249.3 2.7 %all-to-all-done.1 = bf16[8,16,512]{2,1,0:T(8,128)(2,1)S(1)} async-done(((bf16[8,16,512]{2,1,0:T(8,128)(2,1)}), bf16[8,16,512]{2,1,0:T(8,128)(2,1)S(1)}, u32[]{:S(2)}, u32[]{:S(2)}) %all-to-all-start.1) | async-done | bytes 131104 | tf_op jit(solution)/shard_map/all_to_all | solution.py:64
  252.0 0.7 copy.13
Async XLA Ops:
  8.0 40.9 %copy-start = (bf16[1024,512]{1,0:T(8,128)(2,1)S(1)}, bf16[1024,512]{1,0:T(8,128)(2,1)}, u32[]{:S(2)}) copy-start(bf16[1024,512]{1,0:T(8,128)(2,1)} %param.6) | copy-start | bytes 3145732
  8.0 57.8 %all-gather.4.cloned.1.call-start = ((), (), s32[]{:S(2)}) async-start(), calls=%async_computation.6 | async-start | bytes 2228224 | tf_op jit(solution)/shard_map/all_gather | solution.py:14
  8.7 78.9 %reduce-scatter.5.cloned.1.call-start = ((), (), s32[]{:S(2)}) async-start(), calls=%async_computation.9 | async-start | bytes 4718592 | tf_op jit(solution)/shard_map/reduce_scatter | solution.py:39
  47.5 1.4 copy-start.1
  53.2 12.6 %copy-start.4 = (bf16[512,1024]{1,0:T(8,128)(2,1)S(1)}, bf16[512,1024]{1,0:T(8,128)(2,1)}, u32[]{:S(2)}) copy-start(bf16[512,1024]{1,0:T(8,128)(2,1)} %param.5) | copy-start | bytes 3145732
  53.3 73.2 %reduce-scatter.3.cloned.1.call-start = ((), (), s32[]{:S(2)}) async-start(), calls=%async_computation.7 | async-start | bytes 4718592 | tf_op jit(solution)/shard_map/reduce_scatter | solution.py:39
  71.8 93.5 %all-gather.6.cloned.1.call-start = ((), (), s32[]{:S(2)}) async-start(), calls=%async_computation.8 | async-start | bytes 4718592 | tf_op jit(solution)/shard_map/all_gather | solution.py:25
  131.0 68.5 %all-gather.8.cloned.1.call-start = ((), (), s32[]{:S(2)}) async-start(), calls=%async_computation.10 | async-start | bytes 4718592 | tf_op jit(solution)/shard_map/all_gather | solution.py:25
  171.1 35.9 %all-to-all-start = ((bf16[16,128,512]{2,1,0:T(8,128)(2,1)}), bf16[16,128,512]{2,1,0:T(8,128)(2,1)S(1)}, u32[]{:S(2)}, u32[]{:S(2)}) async-start(bf16[16,128,512]{2,1,0:T(8,128)(2,1)} %bitcast.24), calls=%async_computation.1 | async-start | bytes 4194304 | tf_op jit(solution)/shard_map/all_to_all | solution.py:51
  207.1 31.0 %all-to-all-start.3 = ((bf16[16,128,512]{2,1,0:T(8,128)(2,1)}), bf16[16,128,512]{2,1,0:T(8,128)(2,1)}, u32[]{:S(2)}, u32[]{:S(2)}) async-start(bf16[16,128,512]{2,1,0:T(8,128)(2,1)} %bitcast.23), calls=%async_computation.5 | async-start | bytes 4194304 | tf_op jit(solution)/shard_map/all_to_all | solution.py:51
  228.5 0.9 copy-start.3
  229.4 19.2 %copy-start.2 = (bf16[128,512]{1,0:T(8,128)(2,1)S(1)}, bf16[128,512]{1,0:T(8,128)(2,1)}, u32[]{:S(2)}) copy-start(bf16[128,512]{1,0:T(8,128)(2,1)} %param.7) | copy-start | bytes 393220
  238.1 13.9 %all-to-all-start.1 = ((bf16[8,16,512]{2,1,0:T(8,128)(2,1)}), bf16[8,16,512]{2,1,0:T(8,128)(2,1)S(1)}, u32[]{:S(2)}, u32[]{:S(2)}) async-start(bf16[8,16,512]{2,1,0:T(8,128)(2,1)} %bitcast.1), calls=%async_computation.2 | async-start | bytes 262144 | tf_op jit(solution)/shard_map/all_to_all | solution.py:64
Sparse Core Ops, SparseCore 0:
  11.0 54.8 all-gather.3
Sparse Core Ops, SparseCore 1:
  53.4 34.3 reduce-scatter.4
  89.9 36.4 reduce-scatter.2
  131.1 34.1 all-gather.5
  167.6 31.9 all-gather.7
where the time goes:
time: 261 us; the launch traced here: 260 us
  waiting for transfers between devices  136 us (52%)
  blocking collectives  37.6 us (14%)
  matrix products  35.4 us (14%)
  starting transfers between devices  20.9 us (8%)
  between operations  15.7 us (6%)
  other arithmetic  8.13 us (3%)
  local copies, waits for them, and re-layouts  6.64 us (3%)
    all_gather x2, waiting for transfers between devices, hidden_panel(): return lax.all_gather(local_rows, 'col', axis=0, tiled=True)  55.2 us
    reduce_scatter x2, waiting for transfers between devices, width_split(): lax.psum_scatter(term.astype(jnp.bfloat16), 'col', scatter_dimension=0, t...  54.6 us
    all_to_all x1, blocking collectives, token_panel_a2a(): lax.all_to_all(copies, 'row', split_axis=0, concat_axis=0, tiled=True)  37.6 us
    all_gather x1, waiting for transfers between devices, token_panel(): return lax.all_gather(local_rows, 'row', axis=0, tiled=True)  12.5 us
    all_to_all x2, starting transfers between devices, unit_sum(): lax.all_to_all(pieces, 'row', split_axis=0, concat_axis=0, tiled=True)  12.1 us
    dot_general x2, matrix products, contract_last(): lax.dot_general(left, right, (((1,), (1,)), ((), ())), preferred_element_...  10.5 us
    all_to_all x2, waiting for transfers between devices, unit_sum(): lax.all_to_all(pieces, 'row', split_axis=0, concat_axis=0, tiled=True)  9.4 us
    all_to_all x1, starting transfers between devices, local(): lax.all_to_all(block_rows, 'col', split_axis=0, concat_axis=1, tiled=True)  8.57 us
  transfers between devices with their start and end apart: 8, of which 8 were waited for; matrix products, arithmetic and copies ran while one was open for 17% of the time, Pallas kernels for 0%

commit v1 on v0

--- a/solution.py
+++ b/solution.py
@@ -1,7 +1,23 @@
+import functools
 import jax
 import jax.numpy as jnp
 from jax import lax
 from jax.sharding import PartitionSpec as P
+
+
+def fix_zones(mine_x, axis_k):
+    return jnp.concatenate(
+        lax.all_to_all(
+            jnp.stack(lax.axis_size("col") * [mine_x], 0),
+            axis_name="col",
+            split_axis=0,
+            concat_axis=0,
+        ),
+        axis_k,
+    )
+
+
+packet_take = functools.partial(fix_zones, axis_k=0)
 
 
 def gelu_grad(value):
@@ -22,7 +38,7 @@
 
 
 def hidden_panel(local_rows):
-    return lax.all_gather(local_rows, "col", axis=0, tiled=True)
+    return packet_take(local_rows)
 
 
 def contract_last(left, right):

time: 261 us -> 332 us (1.27)
  blocking collectives: 37.6 us -> 93.9 us
  waiting for transfers between devices: 136 us -> 143 us
  starting transfers between devices: 20.9 us -> 26.5 us
  local copies, waits for them, and re-layouts: 6.64 us -> 11 us
    all_to_all x0 -> x1, blocking collectives: none -> 56.3 us  [fix_zones(): lax.all_to_all(jnp.stack(lax.axis_size('col') * [mine_x], 0), axis_name='...]
    all_gather x2 -> x0, waiting for transfers between devices: 55.2 us -> none  [hidden_panel(): return lax.all_gather(local_rows, 'col', axis=0, tiled=True)]
    all_to_all x0 -> x1, waiting for transfers between devices: none -> 43.1 us  [fix_zones(): lax.all_to_all(jnp.stack(lax.axis_size('col') * [mine_x], 0), axis_name='...]
    all_to_all x2, waiting for transfers between devices: 9.4 us -> 27.7 us  [unit_sum(): lax.all_to_all(pieces, 'row', split_axis=0, concat_axis=0, tiled=True)]
    all_to_all x0 -> x1, starting transfers between devices: none -> 5.46 us  [fix_zones(): lax.all_to_all(jnp.stack(lax.axis_size('col') * [mine_x], 0), axis_name='...]
  transfers between devices with their start and end apart: 8 -> 7, of which waited for: 8 -> 7; matrix products, arithmetic and copies ran while one was open for 17% -> 13% of each run, Pallas kernels for 0% -> 0%
where the time goes in v1:
time: 332 us; the launch traced here: 331 us
  waiting for transfers between devices  143 us (43%)
  blocking collectives  93.9 us (28%)
  matrix products  35.6 us (11%)
  starting transfers between devices  26.5 us (8%)
  between operations  15.6 us (5%)
  local copies, waits for them, and re-layouts  11 us (3%)
  other arithmetic  5.76 us (2%)
    all_to_all x1, blocking collectives, fix_zones(): lax.all_to_all(jnp.stack(lax.axis_size('col') * [mine_x], 0), axis_name='...  56.3 us
    reduce_scatter x2, waiting for transfers between devices, width_split(): lax.psum_scatter(term.astype(jnp.bfloat16), 'col', scatter_dimension=0, t...  54.7 us
    all_to_all x1, waiting for transfers between devices, fix_zones(): lax.all_to_all(jnp.stack(lax.axis_size('col') * [mine_x], 0), axis_name='...  43.1 us
    all_to_all x1, blocking collectives, token_panel_a2a(): lax.all_to_all(copies, 'row', split_axis=0, concat_axis=0, tiled=True)  37.6 us
    all_to_all x2, waiting for transfers between devices, unit_sum(): lax.all_to_all(pieces, 'row', split_axis=0, concat_axis=0, tiled=True)  27.7 us
    all_gather x1, waiting for transfers between devices, token_panel(): return lax.all_gather(local_rows, 'row', axis=0, tiled=True)  12.6 us
    all_to_all x2, starting transfers between devices, unit_sum(): lax.all_to_all(pieces, 'row', split_axis=0, concat_axis=0, tiled=True)  11.9 us
    dot_general x2, matrix products, contract_last(): lax.dot_general(left, right, (((1,), (1,)), ((), ())), preferred_element_...  10.6 us
  transfers between devices with their start and end apart: 7, of which 7 were waited for; matrix products, arithmetic and copies ran while one was open for 13% of the time, Pallas kernels for 0%

profile of v1, /device:TPU:1, one launch (start us, length us, event | category | flops | bytes accessed | tf_op | source)
XLA Modules:
  0.0 331.3 jit_solution(14182442566494808253)
XLA Ops:
  8.0 0.0 copy-start
  8.0 0.0 all-gather.2.cloned.1.call-start
  8.1 0.7 all-gather.2.cloned.1.call-update
  8.7 0.0 reduce-scatter.5.cloned.1.call-start
  8.8 1.1 broadcast_in_dim.2
  9.9 37.6 %all_to_all.48 = bf16[16,128,512]{2,1,0:T(8,128)(2,1)S(1)} all-to-all(bf16[16,128,512]{2,1,0:T(8,128)(2,1)S(1)} %broadcast_in_dim.2), channel_id=1, replica_groups=mesh['row'=16,'col'=8] {'row'}, dimensions={0} | all-to-all | bytes 4194304 | tf_op jit(solution)/shard_map/all_to_all | solution.py:37
  47.5 0.0 copy-start.3
  47.5 1.3 copy-done.3
  48.9 0.0 copy-done
  48.9 4.3 %convolution_convert_fusion = bf16[2048,1024]{1,0:T(8,128)(2,1)} fusion(bf16[2048,512]{1,0:T(8,128)(2,1)S(1)} %bitcast.25, bf16[1024,512]{1,0:T(8,128)(2,1)S(1)} %copy-done), kind=kOutput, calls=%fused_computation.2 | convolution fusion | flops 2149580800 | bytes 7340032 | tf_op jit(solution)/shard_map/dot_general | solution.py:45
  53.2 0.0 copy-start.6
  53.2 0.0 reduce-scatter.5.cloned.1.call-update
  53.2 0.0 reduce-scatter.3.cloned.1.call-start
  53.3 12.6 %all-gather.2.cloned.1.call-done = bf16[2048,512]{1,0:T(8,128)(2,1)} async-done(((bf16[128,512]{1,0:T(8,128)(2,1)}), bf16[2048,512]{1,0:T(8,128)(2,1)}) %all-gather.2.cloned.1.call-update) | async-done | bytes 2097168 | tf_op jit(solution)/shard_map/all_gather | solution.py:30
  65.8 0.0 copy-done.6
  65.8 6.0 %convolution_convert_fusion.1 = bf16[2048,1024]{1,0:T(8,128)(2,1)} fusion(bf16[2048,512]{1,0:T(8,128)(2,1)} %all-gather.2.cloned.1.call-done, bf16[512,1024]{1,0:T(8,128)(2,1)S(1)} %copy-done.6), kind=kOutput, calls=%fused_computation.3 | convolution fusion | flops 2149580800 | bytes 7340032 | tf_op jit(solution)/shard_map/dot_general | solution.py:54
  71.8 0.0 reduce-scatter.3.cloned.1.call-update
  71.8 15.8 %reduce-scatter.5.cloned.1.call-done = bf16[256,1024]{1,0:T(8,128)(2,1)} async-done(((bf16[2048,1024]{1,0:T(8,128)(2,1)}), bf16[256,1024]{1,0:T(8,128)(2,1)}) %reduce-scatter.5.cloned.1.call-update) | async-done | bytes 524304 | tf_op jit(solution)/shard_map/reduce_scatter | solution.py:55
  87.6 38.9 %reduce-scatter.3.cloned.1.call-done = bf16[256,1024]{1,0:T(8,128)(2,1)} async-done(((bf16[2048,1024]{1,0:T(8,128)(2,1)}), bf16[256,1024]{1,0:T(8,128)(2,1)}) %reduce-scatter.3.cloned.1.call-update) | async-done | bytes 524304 | tf_op jit(solution)/shard_map/reduce_scatter | solution.py:55
  126.5 3.8 %fusion.38 = (bf16[256,1024]{1,0:T(8,128)(2,1)S(1)}, bf16[256,1024]{1,0:T(8,128)(2,1)S(1)}) fusion(bf16[256,1024]{1,0:T(8,128)(2,1)} %reduce-scatter.3.cloned.1.call-done, bf16[256,1024]{1,0:T(8,128)(2,1)} %reduce-scatter.5.cloned.1.call-done), kind=kLoop, calls=%fused_computation.52 | loop fusion | flops 20185088 | bytes 2097152 | tf_op jit(solution)/shard_map/convert_element_type | solution.py:77
  130.3 0.5 stack.4
  130.8 56.3 %all_to_all.49 = bf16[8,256,1024]{2,1,0:T(8,128)(2,1)} all-to-all(bf16[8,256,1024]{2,1,0:T(8,128)(2,1)S(1)} %stack.4), channel_id=1, replica_groups=mesh['row'=16,'col'=8] {'col'}, dimensions={0} | all-to-all | bytes 8388608 | tf_op jit(solution)/shard_map/all_to_all | solution.py:10
  187.1 2.5 stack.5
  189.6 5.5 %all-to-all-start.4 = ((bf16[8,256,1024]{2,1,0:T(8,128)(2,1)}), bf16[8,256,1024]{2,1,0:T(8,128)(2,1)}, u32[]{:S(2)}, u32[]{:S(2)}) async-start(bf16[8,256,1024]{2,1,0:T(8,128)(2,1)} %stack.5), calls=%async_computation.6 | async-start | bytes 8388608 | tf_op jit(solution)/shard_map/all_to_all | solution.py:10
  195.1 5.8 %convolution_convert_fusion.3 = bf16[2048,512]{1,0:T(8,128)(2,1)} fusion(bf16[2048,1024]{1,0:T(8,128)(2,1)} %bitcast.23, bf16[1024,512]{1,0:T(8,128)(2,1)S(1)} %copy-done), kind=kOutput, calls=%fused_computation.5 | convolution fusion | flops 2148532224 | bytes 7340032 | tf_op jit(solution)/shard_map/dot_general | solution.py:65
  200.9 43.1 %all-to-all-done.4 = bf16[8,256,1024]{2,1,0:T(8,128)(2,1)} async-done(((bf16[8,256,1024]{2,1,0:T(8,128)(2,1)}), bf16[8,256,1024]{2,1,0:T(8,128)(2,1)}, u32[]{:S(2)}, u32[]{:S(2)}) %all-to-all-start.4) | async-done | bytes 4194336 | tf_op jit(solution)/shard_map/all_to_all | solution.py:10
  244.0 6.6 %all-to-all-start.1 = ((bf16[16,128,512]{2,1,0:T(8,128)(2,1)}), bf16[16,128,512]{2,1,0:T(8,128)(2,1)S(1)}, u32[]{:S(2)}, u32[]{:S(2)}) async-start(bf16[16,128,512]{2,1,0:T(8,128)(2,1)} %bitcast.28), calls=%async_computation.2 | async-start | bytes 4194304 | tf_op jit(solution)/shard_map/all_to_all | solution.py:67
  250.6 6.2 %convolution_convert_fusion.2 = bf16[2048,512]{1,0:T(8,128)(2,1)} fusion(bf16[2048,1024]{1,0:T(8,128)(2,1)} %bitcast.5, bf16[512,1024]{1,0:T(8,128)(2,1)} %param.5), kind=kOutput, calls=%fused_computation.4 | convolution fusion | flops 2148532224 | bytes 7340032 | tf_op jit(solution)/shard_map/dot_general | solution.py:45
  256.8 20.2 %all-to-all-done.1 = bf16[16,128,512]{2,1,0:T(8,128)(2,1)S(1)} async-done(((bf16[16,128,512]{2,1,0:T(8,128)(2,1)}), bf16[16,128,512]{2,1,0:T(8,128)(2,1)S(1)}, u32[]{:S(2)}, u32[]{:S(2)}) %all-to-all-start.1) | async-done | bytes 2097184 | tf_op jit(solution)/shard_map/all_to_all | solution.py:67
  277.0 0.0 copy-start.1
  277.1 1.3 copy-done.1
  278.4 5.3 %all-to-all-start.5 = ((bf16[16,128,512]{2,1,0:T(8,128)(2,1)}), bf16[16,128,512]{2,1,0:T(8,128)(2,1)S(1)}, u32[]{:S(2)}, u32[]{:S(2)}) async-start(bf16[16,128,512]{2,1,0:T(8,128)(2,1)} %bitcast.27), calls=%async_computation.7 | async-start | bytes 4194304 | tf_op jit(solution)/shard_map/all_to_all | solution.py:67
  283.7 6.5 %convolution_bitcast_fusion = f32[512,1024]{0,1:T(8,128)} fusion(bf16[2048,1024]{1,0:T(8,128)(2,1)} %bitcast.5, bf16[2048,512]{1,0:T(8,128)(2,1)} %all-gather.2.cloned.1.call-done), kind=kOutput, calls=%fused_computation.12 | convolution fusion | flops 2147483648 | bytes 8388608 | tf_op jit(solution)/shard_map/dot_general | solution.py:84
  290.2 2.9 copy.12
  293.1 0.0 copy-start.2
  293.1 6.7 %fusion.39 = f32[1024,512]{1,0:T(8,128)} fusion(bf16[2048,1024]{1,0:T(8,128)(2,1)} %bitcast.24, bf16[2048,512]{1,0:T(8,128)(2,1)} %bitcast.26), kind=kOutput, calls=%fused_computation.55 | convolution fusion | flops 2147483648 | bytes 8388608 | tf_op jit(solution)/shard_map/dot_general | solution.py:81
  299.8 0.0 copy-done.2
  299.8 0.0 copy-start.5
  299.8 0.3 convert_reduce_fusion.1
  300.1 0.6 copy-done.5
  300.7 0.0 copy-start.4
  300.7 0.7 add_convert_fusion.1
  301.4 7.5 %all-to-all-done.5 = bf16[16,128,512]{2,1,0:T(8,128)(2,1)S(1)} async-done(((bf16[16,128,512]{2,1,0:T(8,128)(2,1)}), bf16[16,128,512]{2,1,0:T(8,128)(2,1)S(1)}, u32[]{:S(2)}, u32[]{:S(2)}) %all-to-all-start.5) | async-done | bytes 2097184 | tf_op jit(solution)/shard_map/all_to_all | solution.py:67
  308.8 9.1 %all-to-all-start.2 = ((bf16[8,16,512]{2,1,0:T(8,128)(2,1)}), bf16[8,16,512]{2,1,0:T(8,128)(2,1)S(1)}, u32[]{:S(2)}, u32[]{:S(2)}) async-start(bf16[8,16,512]{2,1,0:T(8,128)(2,1)} %bitcast.2), calls=%async_computation.3 | async-start | bytes 262144 | tf_op jit(solution)/shard_map/all_to_all | solution.py:80
  317.9 0.3 convert_reduce_fusion
  318.2 0.0 copy-done.4
  318.2 0.7 add_convert_fusion
  318.9 4.3 %all-to-all-done.2 = bf16[8,16,512]{2,1,0:T(8,128)(2,1)S(1)} async-done(((bf16[8,16,512]{2,1,0:T(8,128)(2,1)}), bf16[8,16,512]{2,1,0:T(8,128)(2,1)S(1)}, u32[]{:S(2)}, u32[]{:S(2)}) %all-to-all-start.2) | async-done | bytes 131104 | tf_op jit(solution)/shard_map/all_to_all | solution.py:80
  323.2 0.7 copy.13
Async XLA Ops:
  8.0 40.9 %copy-start = (bf16[1024,512]{1,0:T(8,128)(2,1)S(1)}, bf16[1024,512]{1,0:T(8,128)(2,1)}, u32[]{:S(2)}) copy-start(bf16[1024,512]{1,0:T(8,128)(2,1)} %param.6) | copy-start | bytes 3145732
  8.0 57.8 %all-gather.2.cloned.1.call-start = ((), (), s32[]{:S(2)}) async-start(), calls=%async_computation.8 | async-start | bytes 2228224 | tf_op jit(solution)/shard_map/all_gather | solution.py:30
  8.7 78.9 %reduce-scatter.5.cloned.1.call-start = ((), (), s32[]{:S(2)}) async-start(), calls=%async_computation.10 | async-start | bytes 4718592 | tf_op jit(solution)/shard_map/reduce_scatter | solution.py:55
  47.5 1.3 copy-start.3
  53.2 12.6 %copy-start.6 = (bf16[512,1024]{1,0:T(8,128)(2,1)S(1)}, bf16[512,1024]{1,0:T(8,128)(2,1)}, u32[]{:S(2)}) copy-start(bf16[512,1024]{1,0:T(8,128)(2,1)} %param.5) | copy-start | bytes 3145732
  53.2 73.2 %reduce-scatter.3.cloned.1.call-start = ((), (), s32[]{:S(2)}) async-start(), calls=%async_computation.9 | async-start | bytes 4718592 | tf_op jit(solution)/shard_map/reduce_scatter | solution.py:55
  189.6 54.4 %all-to-all-start.4 = ((bf16[8,256,1024]{2,1,0:T(8,128)(2,1)}), bf16[8,256,1024]{2,1,0:T(8,128)(2,1)}, u32[]{:S(2)}, u32[]{:S(2)}) async-start(bf16[8,256,1024]{2,1,0:T(8,128)(2,1)} %stack.5), calls=%async_computation.6 | async-start | bytes 8388608 | tf_op jit(solution)/shard_map/all_to_all | solution.py:10
  244.0 33.1 %all-to-all-start.1 = ((bf16[16,128,512]{2,1,0:T(8,128)(2,1)}), bf16[16,128,512]{2,1,0:T(8,128)(2,1)S(1)}, u32[]{:S(2)}, u32[]{:S(2)}) async-start(bf16[16,128,512]{2,1,0:T(8,128)(2,1)} %bitcast.28), calls=%async_computation.2 | async-start | bytes 4194304 | tf_op jit(solution)/shard_map/all_to_all | solution.py:67
  277.0 1.3 copy-start.1
  278.4 30.4 %all-to-all-start.5 = ((bf16[16,128,512]{2,1,0:T(8,128)(2,1)}), bf16[16,128,512]{2,1,0:T(8,128)(2,1)S(1)}, u32[]{:S(2)}, u32[]{:S(2)}) async-start(bf16[16,128,512]{2,1,0:T(8,128)(2,1)} %bitcast.27), calls=%async_computation.7 | async-start | bytes 4194304 | tf_op jit(solution)/shard_map/all_to_all | solution.py:67
  293.1 6.7 %copy-start.2 = (bf16[16,128,512]{2,1,0:T(8,128)(2,1)S(1)}, bf16[16,128,512]{2,1,0:T(8,128)(2,1)}, u32[]{:S(2)}) copy-start(bf16[16,128,512]{2,1,0:T(8,128)(2,1)} %copy-done.1) | copy-start | bytes 6291460
  299.8 0.9 copy-start.5
  300.7 17.5 %copy-start.4 = (bf16[128,512]{1,0:T(8,128)(2,1)S(1)}, bf16[128,512]{1,0:T(8,128)(2,1)}, u32[]{:S(2)}) copy-start(bf16[128,512]{1,0:T(8,128)(2,1)} %param.7) | copy-start | bytes 393220
  308.8 14.4 %all-to-all-start.2 = ((bf16[8,16,512]{2,1,0:T(8,128)(2,1)}), bf16[8,16,512]{2,1,0:T(8,128)(2,1)S(1)}, u32[]{:S(2)}, u32[]{:S(2)}) async-start(bf16[8,16,512]{2,1,0:T(8,128)(2,1)} %bitcast.2), calls=%async_computation.3 | async-start | bytes 262144 | tf_op jit(solution)/shard_map/all_to_all | solution.py:80
Sparse Core Ops, SparseCore 0:
  11.0 54.8 all-gather.1
Sparse Core Ops, SparseCore 1:
  53.3 34.3 reduce-scatter.4
  89.9 36.5 reduce-scatter.2
